TPU v7x, 128 devices: a whole 4x4x4 slice. The times are simulated.
128 devices in a mesh: leaf: 4 (over x_lo, core), row: 8 (over x_hi, y), col: 4 (over z).
Axes of the slice: x: 4 (x_hi: 2, x_lo: 2; x = x_hi * 2 + x_lo), y: 4, z: 4, core: 2. Of those that a mesh axis runs over, the one named last changes fastest.
Arguments:
- parent_adj: float32 [16384, 16384], P(('leaf', 'row'), 'col'), may hold values from -70 to 70, as said below
- child_map: int32 [4, 8], replicated, may hold values from 0 to 127, as said below
- lower_panel: float32 [4, 1024, 4096], P('leaf', 'col', 'row'), may hold values from -0.09375 to 0.09375
- pivot_inverse: float32 [4, 4096, 4096], P('leaf', 'row', 'col'), may hold values from -1 to 3, as said below
Outputs:
- update_adj: float32 [4, 1024, 1024], P('leaf', 'row', 'col')
- off_adj: float32 [4, 1024, 4096], P('leaf', 'row', 'col')
- pivot_adj: float32 [4, 4096, 4096], P('leaf', 'row', 'col')
Inputs may be any that keep to these rules, and one draw needn't show every extreme that they name: `child_map`: each row lists 8 distinct parent block ids in increasing order; every row contains block 0 and block 127. parent_adj is symmetric. Each pivot_inverse[c] is lower triangular with diagonal entries of 1 to 3.
All inputs are finite; a program needn't handle non-finite values.
Results may differ from a plain program's by a relative error of at most 0.0003.
Values sent between devices are 32-bit elements; how exact they have to be, the bound alone decides.
A program may use at most 128 MiB of HBM per device.

v0:
```python
import jax
import jax.numpy as jnp
from jax import lax
from jax.sharding import PartitionSpec as P

BLK = 128
exact_mode = lax.Precision.HIGHEST


def take_child(blocks_view, block_ids):
    return jnp.take(blocks_view, block_ids, axis=0)


def shards(parent_adj, child_map, lower_panel, pivot_inverse):
    row_count = lax.axis_size("row")
    column_count = lax.axis_size("col")
    leaf_index = lax.axis_index("leaf")
    row_index = lax.axis_index("row")
    column_index = lax.axis_index("col")
    children = child_map.shape[0]
    blocks_all = child_map.shape[1]
    local_rows = parent_adj.shape[0]
    local_columns = parent_adj.shape[1]
    row_blocks = local_rows // BLK
    column_blocks = local_columns // BLK
    per_column = blocks_all // column_count
    per_row = blocks_all // row_count
    width = per_column * BLK
    column_ids = jnp.transpose(child_map.reshape(children, column_count, per_column), (1, 0, 2))
    column_local = column_ids - column_index * column_blocks
    column_owned = (column_local >= 0) & (column_local < column_blocks)
    column_safe = jnp.clip(column_local, 0, column_blocks - 1)
    parent_view = parent_adj.reshape(local_rows, column_blocks, BLK)
    picked = jnp.take(parent_view, column_safe.reshape(-1), axis=1)
    picked = picked.reshape(local_rows, column_count, children, per_column, BLK)
    picked = jnp.where(column_owned[None, :, :, :, None], picked, 0.0)
    picked = picked.reshape(local_rows, column_count, children * width)
    columns_kept = lax.psum_scatter(picked, "col", scatter_dimension=1, tiled=True)
    selected = columns_kept.reshape(row_blocks, BLK, children, width)
    by_child = jnp.moveaxis(selected, 2, 0)
    owner = leaf_index * row_count + row_index
    row_local = child_map - owner * row_blocks
    row_owned = (row_local >= 0) & (row_local < row_blocks)
    row_safe = jnp.clip(row_local, 0, row_blocks - 1)
    contribution = jax.vmap(take_child)(by_child, row_safe)
    contribution = jnp.where(row_owned[:, :, None, None], contribution, 0.0)
    update = lax.psum_scatter(
        contribution.reshape(children * row_count * per_row * BLK, width),
        ("leaf", "row"),
        scatter_dimension=0,
        tiled=True,
    )
    lower = lower_panel[0]
    inverse = pivot_inverse[0]
    lower_all = lax.all_gather(lower, "col", axis=0, tiled=True)
    factor = lax.psum_scatter(
        jnp.dot(lower_all, inverse, precision=exact_mode, preferred_element_type=jnp.float32),
        "row",
        scatter_dimension=0,
        tiled=True,
    )
    update_all = lax.all_gather(update, "col", axis=1, tiled=True)
    carried = jnp.dot(
        update_all,
        lax.all_gather(factor, "row", axis=0, tiled=True),
        precision=exact_mode,
        preferred_element_type=jnp.float32,
    )
    factor_all, inverse_all = (
        lax.all_gather(factor, "col", axis=1, tiled=True),
        lax.all_gather(inverse, "col", axis=1, tiled=True),
    )
    first = jnp.dot(factor_all.T, carried, precision=exact_mode, preferred_element_type=jnp.float32)
    second = jnp.dot(
        inverse_all.T, inverse, precision=exact_mode, preferred_element_type=jnp.float32
    )
    pivot = lax.psum_scatter(first + second, "row", scatter_dimension=0, tiled=True)
    return (update[None], (-2.0 * carried)[None], pivot[None])


def solution(mesh):
    in_specs = (P(("leaf", "row"), "col"), P(), P("leaf", "col", "row"), P("leaf", "row", "col"))
    out_specs = (P("leaf", "row", "col"), P("leaf", "row", "col"), P("leaf", "row", "col"))
    return jax.shard_map(shards, mesh=mesh, in_specs=in_specs, out_specs=out_specs, check_vma=False)
```

profile of v0, /device:TPU:2, one launch (start us, length us, event | category | flops | bytes accessed | tf_op | source)
XLA Modules:
  0.0 789.7 jit_solution(10354824878462700312)
XLA Ops:
  7.2 0.0 all-gather.11.cloned.1.call-start
  7.2 0.7 all-gather.11.cloned.1.call-update
  7.9 0.0 reduce-scatter.5.cloned.1.call-start
  7.9 0.7 subtract_clamp_fusion
  8.6 0.1 copy.40
  8.7 0.1 copy.43
  8.8 0.1 copy.41
  9.0 0.1 broadcast_in_dim.82
  9.1 0.7 compare_and_fusion.3
  9.8 0.1 and.31
  9.9 0.1 broadcast_in_dim.79
  10.0 9.0 %copy.42 = f32[512,4096]{0,1:T(8,128)} copy(f32[512,4096]{1,0:T(8,128)} %param.4) | data formatting | bytes 16777216 | tf_op args[0]
  19.0 9.0 %copy.44 = f32[512,32,128]{2,0,1:T(8,128)} copy(f32[512,32,128]{0,2,1:T(8,128)} %bitcast.49) | data formatting | bytes 16777216 | tf_op jit(solution)/shard_map/reshape | solution.py:33
  28.0 0.1 reshape.79
  28.1 7.8 gather_fusion
  35.9 9.0 %copy.45 = f32[512,32,128]{0,2,1:T(8,128)} copy(f32[512,32,128]{2,0,1:T(8,128)} %bitcast.47) | data formatting | bytes 16777216 | tf_op jit(solution)/shard_map/jit(_take)/gather | solution.py:34
  44.9 7.4 fusion.2
  52.4 0.0 copy-start
  52.4 0.0 reduce-scatter.5.cloned.1.call-update
  52.4 0.0 reduce-scatter.9.cloned.1.call-start
  52.5 0.0 all-gather.11.cloned.1.call-done
  52.5 1.5 copy-done
  54.0 9.7 %fusion.5 = f32[1024,1024]{1,0:T(8,128)} fusion(f32[1,512,1024]{2,1,0:T(8,128)S(1)} %copy-done, f32[1,1024,512]{2,1,0:T(8,128)} %all-gather.11.cloned.1.call-done), kind=kOutput, calls=%fused_computation.10 | convolution fusion | flops 6442450944 | bytes 8388608 | tf_op jit(solution)/shard_map/dot_general | solution.py:57
  63.7 0.0 copy-start.2
  63.7 0.0 reduce-scatter.9.cloned.1.call-update
  63.7 0.0 all-gather.13.cloned.1.call-start
  63.8 0.5 all-gather.13.cloned.1.call-update
  64.3 0.0 reduce-scatter.7.cloned.1.call-start
  64.3 0.0 copy-done.2
  64.4 0.1 reshape.89
  64.5 0.1 broadcast_bitcast_fusion
  64.5 71.2 %reduce-scatter.5.cloned.1.call-done = f32[512,1,1024]{0,2,1:T(8,128)} async-done(((f32[512,4,1024]{0,2,1:T(8,128)}), f32[512,1,1024]{0,2,1:T(8,128)}) %reduce-scatter.5.cloned.1.call-update) | async-done | bytes 2097168 | tf_op jit(solution)/shard_map/reduce_scatter | solution.py:38
  135.7 2.9 reshape.103
  138.6 1.9 copy.47
  140.5 2.8 gather_fusion.1
  143.3 6.8 fusion.3
  150.0 0.0 copy-start.1
  150.0 0.0 reduce-scatter.7.cloned.1.call-update
  150.1 0.0 all-gather.7.cloned.1.call-start
  150.1 72.6 %reduce-scatter.9.cloned.1.call-done = f32[128,1024]{1,0:T(8,128)} async-done(((f32[1024,1024]{1,0:T(8,128)}), f32[128,1024]{1,0:T(8,128)}) %reduce-scatter.9.cloned.1.call-update) | async-done | bytes 524304 | tf_op jit(solution)/shard_map/reduce_scatter | solution.py:56
  222.7 0.0 all-gather.7.cloned.1.call-update
  222.7 0.0 all-gather.9.cloned.1.call-start
  222.8 0.7 all-gather.9.cloned.1.call-update
  223.5 0.2 reduce-scatter.11.cloned.1.call-start
  223.7 83.7 %all-gather.13.cloned.1.call-done = f32[1,512,4096]{2,1,0:T(8,128)} async-done(((f32[1,512,1024]{2,1,0:T(8,128)}), f32[1,512,4096]{2,1,0:T(8,128)}) %all-gather.13.cloned.1.call-update) | async-done | bytes 8388624 | tf_op jit(solution)/shard_map/all_gather | solution.py:71
  307.4 0.0 copy-done.1
  307.4 30.7 %fusion = f32[4096,1024]{1,0:T(8,128)} fusion(f32[1,512,4096]{2,1,0:T(8,128)} %all-gather.13.cloned.1.call-done, f32[1,512,1024]{2,1,0:T(8,128)S(1)} %copy-done.1), kind=kOutput, calls=%fused_computation.3 | convolution fusion | flops 25769803776 | bytes 27262976 | tf_op jit(solution)/shard_map/dot_general | solution.py:74
  338.1 125.8 %reduce-scatter.7.cloned.1.call-done = f32[128,256]{1,0:T(8,128)} async-done(((f32[4096,256]{1,0:T(8,128)}), f32[128,256]{1,0:T(8,128)}) %reduce-scatter.7.cloned.1.call-update) | async-done | bytes 131088 | tf_op jit(solution)/shard_map/reduce_scatter | solution.py:47
  463.9 13.5 %all_gather.15 = f32[128,1024]{1,0:T(8,128)S(1)} all-gather(f32[128,256]{1,0:T(8,128)} %reduce-scatter.7.cloned.1.call-done), channel_id=1, replica_groups=mesh['leaf'=4,'row'=8,'col'=4] {'col'}, dimensions={1}, use_global_device_ids=true | all-gather | bytes 655360 | tf_op jit(solution)/shard_map/all_gather | solution.py:62
  477.4 62.9 %all-gather.7.cloned.1.call-done = f32[1024,1024]{1,0:T(8,128)} async-done(((f32[128,1024]{1,0:T(8,128)}), f32[1024,1024]{1,0:T(8,128)}) %all-gather.7.cloned.1.call-update) | async-done | bytes 4194320 | tf_op jit(solution)/shard_map/all_gather | solution.py:65
  540.2 4.6 fusion.9
  544.8 27.1 %all-gather.9.cloned.1.call-done = f32[128,4096]{1,0:T(8,128)} async-done(((f32[128,1024]{1,0:T(8,128)}), f32[128,4096]{1,0:T(8,128)}) %all-gather.9.cloned.1.call-update) | async-done | bytes 2097168 | tf_op jit(solution)/shard_map/all_gather | solution.py:70
  571.9 19.1 %convolution_add_fusion = f32[4096,1024]{1,0:T(8,128)} fusion(f32[4096,1024]{1,0:T(8,128)} %fusion, f32[128,4096]{1,0:T(8,128)} %all-gather.9.cloned.1.call-done, f32[128,1024]{1,0:T(8,128)S(1)} %fusion.9), kind=kOutput, calls=%fused_computation.2 | convolution fusion | flops 6446645248 | bytes 36175872 | tf_op jit(solution)/shard_map/dot_general | solution.py:73
  591.0 0.0 reduce-scatter.11.cloned.1.call-update
  591.0 0.8 multiply_bitcast_fusion
  591.8 191.0 %reduce-scatter.11.cloned.1.call-done = f32[512,1024]{1,0:T(8,128)} async-done(((f32[4096,1024]{1,0:T(8,128)}), f32[512,1024]{1,0:T(8,128)}) %reduce-scatter.11.cloned.1.call-update) | async-done | bytes 2097168 | tf_op jit(solution)/shard_map/reduce_scatter | solution.py:77
  (7 shorter events, 0.1 us)
Async XLA Ops:
  7.2 45.3 %all-gather.11.cloned.1.call-start = ((), (), s32[]{:S(2)}) async-start(), calls=%async_computation.10 | async-start | bytes 2621440 | tf_op jit(solution)/shard_map/all_gather | solution.py:55
  7.9 127.8 %reduce-scatter.5.cloned.1.call-start = ((), (), s32[]{:S(2)}) async-start(), calls=%async_computation.4 | async-start | bytes 10485760 | tf_op jit(solution)/shard_map/reduce_scatter | solution.py:38
  52.4 1.6 copy-start
  52.4 170.3 %reduce-scatter.9.cloned.1.call-start = ((), (), s32[]{:S(2)}) async-start(), calls=%async_computation.6 | async-start | bytes 4718592 | tf_op jit(solution)/shard_map/reduce_scatter | solution.py:56
  63.7 0.7 copy-start.2
  63.7 243.7 %all-gather.13.cloned.1.call-start = ((), (), s32[]{:S(2)}) async-start(), calls=%async_computation.11 | async-start | bytes 10485760 | tf_op jit(solution)/shard_map/all_gather | solution.py:71
  64.3 399.6 %reduce-scatter.7.cloned.1.call-start = ((), (), s32[]{:S(2)}) async-start(), calls=%async_computation.5 | async-start | bytes 4325376 | tf_op jit(solution)/shard_map/reduce_scatter | solution.py:47
  150.0 157.4 %copy-start.1 = (f32[1,512,1024]{2,1,0:T(8,128)S(1)}, f32[1,512,1024]{2,1,0:T(8,128)}, u32[]{:S(2)}) copy-start(f32[1,512,1024]{2,1,0:T(8,128)} %param.7) | copy-start | bytes 6291460
  150.1 390.2 %all-gather.7.cloned.1.call-start = ((), (), s32[]{:S(2)}) async-start(), calls=%async_computation.7 | async-start | bytes 4718592 | tf_op jit(solution)/shard_map/all_gather | solution.py:65
  222.7 349.2 %all-gather.9.cloned.1.call-start = ((), (), s32[]{:S(2)}) async-start(), calls=%async_computation.8 | async-start | bytes 2621440 | tf_op jit(solution)/shard_map/all_gather | solution.py:70
  223.5 559.4 %reduce-scatter.11.cloned.1.call-start = ((), (), s32[]{:S(2)}) async-start(), calls=%async_computation.9 | async-start | bytes 18874368 | tf_op jit(solution)/shard_map/reduce_scatter | solution.py:77
Sparse Core Ops, SparseCore 0:
  9.7 33.4 all-gather.10
  52.5 83.1 reduce-scatter.4
  139.5 83.1 reduce-scatter.8
  224.3 83.0 all-gather.12
  310.4 153.4 reduce-scatter.6
  466.4 73.7 all-gather.6
  542.0 29.8 all-gather.8
  591.1 191.6 reduce-scatter.10
where the time goes:
time: 791 us; the launch traced here: 790 us
  waiting for transfers between devices  636 us (80%)
  matrix products  64 us (8%)
  local copies, waits for them, and re-layouts  44.8 us (6%)
  other arithmetic  16.5 us (2%)
  between operations  14.2 us (2%)
  blocking collectives  13.5 us (2%)
    reduce_scatter x1, waiting for transfers between devices, shards(): lax.psum_scatter(first + second, 'row', scatter_dimension=0, tiled=True)  191 us
    reduce_scatter x1, waiting for transfers between devices, shards(): lax.psum_scatter(contribution.reshape(children * row_count * per_row * BL...  126 us
    all_gather x1, waiting for transfers between devices, shards(): lax.all_gather(inverse, 'col', axis=1, tiled=True)  83.7 us
    reduce_scatter x1, waiting for transfers between devices, shards(): lax.psum_scatter(jnp.dot(lower_all, inverse, precision=exact_mode, prefer...  72.6 us
    reduce_scatter x1, waiting for transfers between devices, shards(): lax.psum_scatter(picked, 'col', scatter_dimension=1, tiled=True)  71.2 us
    all_gather x1, waiting for transfers between devices, shards(): lax.all_gather(factor, 'row', axis=0, tiled=True)  62.9 us
    dot_general x1, matrix products, shards(): jnp.dot(inverse_all.T, inverse, precision=exact_mode, preferred_element_t...  30.7 us
    all_gather x1, waiting for transfers between devices, shards(): lax.all_gather(factor, 'col', axis=1, tiled=True)  27.1 us
  transfers between devices with their start and end apart: 8, of which 7 were waited for; matrix products, arithmetic and copies ran while one was open for 13% of the time, Pallas kernels for 0%

commit v1 on v0

--- a/solution.py
+++ b/solution.py
@@ -5,6 +5,11 @@
 
 BLK = 128
 exact_mode = lax.Precision.HIGHEST
+
+
+def gather_by_exchange(x, axis, dim):
+    copies = jnp.concatenate([x] * lax.axis_size(axis), axis=dim)
+    return lax.all_to_all(copies, axis, dim, dim, tiled=True)
 
 
 def take_child(blocks_view, block_ids):
@@ -68,7 +73,7 @@
     )
     factor_all, inverse_all = (
         lax.all_gather(factor, "col", axis=1, tiled=True),
-        lax.all_gather(inverse, "col", axis=1, tiled=True),
+        gather_by_exchange(inverse, "col", 1),
     )
     first = jnp.dot(factor_all.T, carried, precision=exact_mode, preferred_element_type=jnp.float32)
     second = jnp.dot(

time: 791 us -> 705 us (0.89)
  waiting for transfers between devices: 636 us -> 530 us
  local copies, waits for them, and re-layouts: 44.8 us -> 58.5 us
    reduce_scatter x1, waiting for transfers between devices: 126 us -> 12.2 us  [shards(): lax.psum_scatter(contribution.reshape(children * row_count * per_row * BL...]
    all_to_all x0 -> x1, waiting for transfers between devices: none -> 92.3 us  [gather_by_exchange(): return lax.all_to_all(copies, axis, dim, dim, tiled=True)]
    all_gather x1 -> x0, waiting for transfers between devices: 83.7 us -> none  [shards(): lax.all_gather(inverse, 'col', axis=1, tiled=True)]
    all_to_all x0 -> x1, local copies, waits for them, and re-layouts: none -> 8.75 us  [gather_by_exchange(): return lax.all_to_all(copies, axis, dim, dim, tiled=True)]
  transfers between devices with their start and end apart: 8 -> 8, of which waited for: 7 -> 7; matrix products, arithmetic and copies ran while one was open for 13% -> 17% of each run, Pallas kernels for 0% -> 0%
where the time goes in v1:
time: 705 us; the launch traced here: 704 us
  waiting for transfers between devices  530 us (75%)
  matrix products  64.4 us (9%)
  local copies, waits for them, and re-layouts  58.5 us (8%)
  other arithmetic  16.5 us (2%)
  between operations  14.2 us (2%)
  blocking collectives  13.6 us (2%)
    reduce_scatter x1, waiting for transfers between devices, shards(): lax.psum_scatter(first + second, 'row', scatter_dimension=0, tiled=True)  191 us
    all_to_all x1, waiting for transfers between devices, gather_by_exchange(): return lax.all_to_all(copies, axis, dim, dim, tiled=True)  92.3 us
    reduce_scatter x1, waiting for transfers between devices, shards(): lax.psum_scatter(jnp.dot(lower_all, inverse, precision=exact_mode, prefer...  72.6 us
    reduce_scatter x1, waiting for transfers between devices, shards(): lax.psum_scatter(picked, 'col', scatter_dimension=1, tiled=True)  71.2 us
    all_gather x1, waiting for transfers between devices, shards(): lax.all_gather(factor, 'row', axis=0, tiled=True)  62.8 us
    dot_general x1, matrix products, shards(): jnp.dot(inverse_all.T, inverse, precision=exact_mode, preferred_element_t...  31 us
    all_gather x1, waiting for transfers between devices, shards(): lax.all_gather(factor, 'col', axis=1, tiled=True)  26.9 us
    dot_general x1, matrix products, shards(): jnp.dot(factor_all.T, carried, precision=exact_mode, preferred_element_ty...  19.1 us
  transfers between devices with their start and end apart: 8, of which 7 were waited for; matrix products, arithmetic and copies ran while one was open for 17% of the time, Pallas kernels for 0%

profile of v1, /device:TPU:2, one launch (start us, length us, event | category | flops | bytes accessed | tf_op | source)
XLA Modules:
  0.0 703.7 jit_solution(7973748699754651959)
XLA Ops:
  7.2 0.0 all-gather.9.cloned.1.call-start
  7.2 0.7 all-gather.9.cloned.1.call-update
  7.9 0.0 reduce-scatter.5.cloned.1.call-start
  7.9 0.7 subtract_clamp_fusion
  8.6 0.1 copy.69
  8.7 0.1 copy.72
  8.8 0.1 copy.70
  9.0 0.1 broadcast_in_dim.82
  9.1 0.7 compare_and_fusion.3
  9.8 0.1 and.31
  9.9 0.1 broadcast_in_dim.79
  10.0 9.0 %copy.71 = f32[512,4096]{0,1:T(8,128)} copy(f32[512,4096]{1,0:T(8,128)} %param.4) | data formatting | bytes 16777216 | tf_op args[0]
  19.0 9.0 %copy.73 = f32[512,32,128]{2,0,1:T(8,128)} copy(f32[512,32,128]{0,2,1:T(8,128)} %bitcast.49) | data formatting | bytes 16777216 | tf_op jit(solution)/shard_map/reshape | solution.py:38
  28.0 0.1 reshape.91
  28.2 7.8 %gather_fusion = f32[32,512,128]{2,1,0:T(8,128)} fusion(f32[512,32,128]{2,0,1:T(8,128)} %copy.73, s32[1024]{0:T(1024)S(1)} %pad_clamp_fusion), kind=kCustom, calls=%fused_computation | custom fusion | bytes 16777344 | tf_op jit(solution)/shard_map/jit(_take)/gather | solution.py:39
  35.9 9.0 %copy.74 = f32[512,32,128]{0,2,1:T(8,128)} copy(f32[512,32,128]{2,0,1:T(8,128)} %bitcast.47) | data formatting | bytes 16777216 | tf_op jit(solution)/shard_map/jit(_take)/gather | solution.py:39
  44.9 7.4 %fusion = f32[512,4,1024]{0,2,1:T(8,128)} fusion(pred[4,1024]{1,0:T(4,128)(4,1)S(1)} %broadcast_in_dim.83, pred[4,1024]{1,0:T(4,128)(4,1)S(1)} %broadcast_in_dim.80, f32[512,4,1024]{0,2,1:T(8,128)} %bitcast.48), kind=kLoop, calls=%fused_computation.4 | loop fusion | flops 4194304 | bytes 16785408 | tf_op jit(solution)/shard_map/jit(_where)/select_n | solution.py:41
  52.4 0.0 copy-start
  52.4 0.0 reduce-scatter.5.cloned.1.call-update
  52.4 0.0 reduce-scatter.9.cloned.1.call-start
  52.5 0.0 all-gather.9.cloned.1.call-done
  52.5 1.5 copy-done
  54.0 9.7 %fusion.2 = f32[1024,1024]{1,0:T(8,128)} fusion(f32[1,1024,512]{2,1,0:T(8,128)} %all-gather.9.cloned.1.call-done, f32[1,512,1024]{2,1,0:T(8,128)S(1)} %copy-done), kind=kOutput, calls=%fused_computation.7 | convolution fusion | flops 6442450944 | bytes 8388608 | tf_op jit(solution)/shard_map/dot_general | solution.py:62
  63.7 0.0 copy-start.2
  63.7 0.0 reduce-scatter.9.cloned.1.call-update
  63.7 0.0 reduce-scatter.7.cloned.1.call-start
  63.8 0.6 copy-done.2
  64.4 0.1 reshape.101
  64.5 0.1 broadcast_bitcast_fusion
  64.5 71.2 %reduce-scatter.5.cloned.1.call-done = f32[512,1,1024]{0,2,1:T(8,128)} async-done(((f32[512,4,1024]{0,2,1:T(8,128)}), f32[512,1,1024]{0,2,1:T(8,128)}) %reduce-scatter.5.cloned.1.call-update) | async-done | bytes 2097168 | tf_op jit(solution)/shard_map/reduce_scatter | solution.py:43
  135.7 2.9 reshape.114
  138.6 1.9 copy.76
  140.5 2.8 gather_fusion.1
  143.3 6.8 fusion.1
  150.1 0.0 copy-start.1
  150.1 0.0 reduce-scatter.7.cloned.1.call-update
  150.1 0.0 all-gather.5.cloned.1.call-start
  150.2 72.6 %reduce-scatter.9.cloned.1.call-done = f32[128,1024]{1,0:T(8,128)} async-done(((f32[1024,1024]{1,0:T(8,128)}), f32[128,1024]{1,0:T(8,128)}) %reduce-scatter.9.cloned.1.call-update) | async-done | bytes 524304 | tf_op jit(solution)/shard_map/reduce_scatter | solution.py:61
  222.7 0.0 all-gather.5.cloned.1.call-update
  222.8 0.0 copy-done.1
  222.8 4.3 concatenate.4
  227.1 5.6 all-to-all-start
  232.7 0.0 all-gather.7.cloned.1.call-start
  232.8 0.5 all-gather.7.cloned.1.call-update
  233.3 0.2 reduce-scatter.11.cloned.1.call-start
  233.5 92.3 %all-to-all-done = f32[512,4,1024]{2,0,1:T(8,128)} async-done(((f32[512,4,1024]{2,0,1:T(8,128)}), f32[512,4,1024]{2,0,1:T(8,128)}, u32[]{:S(2)}, u32[]{:S(2)}) %all-to-all-start) | async-done | bytes 8388640 | tf_op jit(solution)/shard_map/all_to_all | solution.py:12
  325.8 8.8 %copy.77 = f32[512,4,1024]{0,2,1:T(8,128)} copy(f32[512,4,1024]{2,0,1:T(8,128)} %all-to-all-done) | data formatting | bytes 16777216 | tf_op jit(solution)/shard_map/all_to_all | solution.py:12
  334.6 31.0 %fusion.5 = f32[4096,1024]{1,0:T(8,128)} fusion(f32[512,4096]{0,1:T(8,128)} %bitcast.46, f32[1,512,1024]{2,1,0:T(8,128)S(1)} %copy-done.1), kind=kOutput, calls=%fused_computation.23 | convolution fusion | flops 25769803776 | bytes 27262976 | tf_op jit(solution)/shard_map/dot_general | solution.py:79
  365.6 12.2 %reduce-scatter.7.cloned.1.call-done = f32[128,256]{1,0:T(8,128)} async-done(((f32[4096,256]{1,0:T(8,128)}), f32[128,256]{1,0:T(8,128)}) %reduce-scatter.7.cloned.1.call-update) | async-done | bytes 131088 | tf_op jit(solution)/shard_map/reduce_scatter | solution.py:52
  377.8 13.6 %all_gather.12 = f32[128,1024]{1,0:T(8,128)S(1)} all-gather(f32[128,256]{1,0:T(8,128)} %reduce-scatter.7.cloned.1.call-done), channel_id=1, replica_groups=mesh['leaf'=4,'row'=8,'col'=4] {'col'}, dimensions={1}, use_global_device_ids=true | all-gather | bytes 655360 | tf_op jit(solution)/shard_map/all_gather | solution.py:67
  391.5 62.8 %all-gather.5.cloned.1.call-done = f32[1024,1024]{1,0:T(8,128)} async-done(((f32[128,1024]{1,0:T(8,128)}), f32[1024,1024]{1,0:T(8,128)}) %all-gather.5.cloned.1.call-update) | async-done | bytes 4194320 | tf_op jit(solution)/shard_map/all_gather | solution.py:70
  454.3 4.6 fusion.8
  458.9 26.9 %all-gather.7.cloned.1.call-done = f32[128,4096]{1,0:T(8,128)} async-done(((f32[128,1024]{1,0:T(8,128)}), f32[128,4096]{1,0:T(8,128)}) %all-gather.7.cloned.1.call-update) | async-done | bytes 2097168 | tf_op jit(solution)/shard_map/all_gather | solution.py:75
  485.8 19.1 %convolution_add_fusion = f32[4096,1024]{1,0:T(8,128)} fusion(f32[4096,1024]{1,0:T(8,128)} %fusion.5, f32[128,4096]{1,0:T(8,128)} %all-gather.7.cloned.1.call-done, f32[128,1024]{1,0:T(8,128)S(1)} %fusion.8), kind=kOutput, calls=%fused_computation.2 | convolution fusion | flops 6446645248 | bytes 36175872 | tf_op jit(solution)/shard_map/dot_general | solution.py:78
  504.9 0.0 reduce-scatter.11.cloned.1.call-update
  504.9 0.8 multiply_bitcast_fusion
  505.7 191.1 %reduce-scatter.11.cloned.1.call-done = f32[512,1024]{1,0:T(8,128)} async-done(((f32[4096,1024]{1,0:T(8,128)}), f32[512,1024]{1,0:T(8,128)}) %reduce-scatter.11.cloned.1.call-update) | async-done | bytes 2097168 | tf_op jit(solution)/shard_map/reduce_scatter | solution.py:82
  (7 shorter events, 0.1 us)
Async XLA Ops:
  7.2 45.3 %all-gather.9.cloned.1.call-start = ((), (), s32[]{:S(2)}) async-start(), calls=%async_computation.11 | async-start | bytes 2621440 | tf_op jit(solution)/shard_map/all_gather | solution.py:60
  7.9 127.8 %reduce-scatter.5.cloned.1.call-start = ((), (), s32[]{:S(2)}) async-start(), calls=%async_computation.5 | async-start | bytes 10485760 | tf_op jit(solution)/shard_map/reduce_scatter | solution.py:43
  52.4 1.6 copy-start
  52.4 170.3 %reduce-scatter.9.cloned.1.call-start = ((), (), s32[]{:S(2)}) async-start(), calls=%async_computation.7 | async-start | bytes 4718592 | tf_op jit(solution)/shard_map/reduce_scatter | solution.py:61
  63.7 0.7 copy-start.2
  63.7 314.1 %reduce-scatter.7.cloned.1.call-start = ((), (), s32[]{:S(2)}) async-start(), calls=%async_computation.6 | async-start | bytes 4325376 | tf_op jit(solution)/shard_map/reduce_scatter | solution.py:52
  150.1 72.7 %copy-start.1 = (f32[1,512,1024]{2,1,0:T(8,128)S(1)}, f32[1,512,1024]{2,1,0:T(8,128)}, u32[]{:S(2)}) copy-start(f32[1,512,1024]{2,1,0:T(8,128)} %param.7) | copy-start | bytes 6291460
  150.1 304.2 %all-gather.5.cloned.1.call-start = ((), (), s32[]{:S(2)}) async-start(), calls=%async_computation.8 | async-start | bytes 4718592 | tf_op jit(solution)/shard_map/all_gather | solution.py:70
  227.1 98.7 %all-to-all-start = ((f32[512,4,1024]{2,0,1:T(8,128)}), f32[512,4,1024]{2,0,1:T(8,128)}, u32[]{:S(2)}, u32[]{:S(2)}) async-start(f32[512,4,1024]{2,0,1:T(8,128)} %concatenate.4), calls=%async_computation.3 | async-start | bytes 16777216 | tf_op jit(solution)/shard_map/all_to_all | solution.py:12
  232.7 253.1 %all-gather.7.cloned.1.call-start = ((), (), s32[]{:S(2)}) async-start(), calls=%async_computation.9 | async-start | bytes 2621440 | tf_op jit(solution)/shard_map/all_gather | solution.py:75
  233.3 463.5 %reduce-scatter.11.cloned.1.call-start = ((), (), s32[]{:S(2)}) async-start(), calls=%async_computation.10 | async-start | bytes 18874368 | tf_op jit(solution)/shard_map/reduce_scatter | solution.py:82
Sparse Core Ops, SparseCore 0:
  9.7 33.4 all-gather.8
  52.5 83.1 reduce-scatter.4
  139.5 83.1 reduce-scatter.8
  225.7 152.0 reduce-scatter.6
  380.3 73.9 all-gather.4
  455.9 29.8 all-gather.6
  505.0 191.7 reduce-scatter.10
